TPU v7x, 32 devices: a whole 2x2x4 slice. The times are simulated.
32 devices in a mesh: dp: 4 (over z), expert: 8 (over y, x, core).
Axes of the slice: x: 2, y: 2, z: 4, core: 2. Of those that a mesh axis runs over, the one named last changes fastest.
Arguments:
- tokens: bfloat16 [256, 3584], P(('dp', 'expert')), may hold values from -6 to 6
- routes: int32 [256, 8], P(('dp', 'expert')), may hold values from 0 to 63, as said below
- gate_values: bfloat16 [256, 8], P(('dp', 'expert')), may hold values from 0.099609375 to 0.5
- expert_map: int32 [64], replicated, may hold values from 0 to 63, as said below
- row_counts: int32 [32], P(('dp', 'expert')), may hold values from 1 to 8, 224 in all
- gate_weight: bfloat16 [8, 3584, 2048], P('expert', None, 'dp'), may hold values from -0.09375 to 0.09375
- up_weight: bfloat16 [8, 3584, 2048], P('expert', None, 'dp'), may hold values from -0.09375 to 0.09375
- down_weight: bfloat16 [8, 2048, 3584], P('expert', 'dp'), may hold values from -0.125 to 0.125
- delta_in: bfloat16 [8, 8, 3584, 256], P('expert', 'dp'), may hold values from -0.09375 to 0.09375
- delta_out: bfloat16 [8, 8, 256, 3584], P('expert', 'dp'), may hold values from -0.375 to 0.375
Outputs:
- mixed: bfloat16 [256, 3584], P(('dp', 'expert'))
Inputs may be any that keep to these rules, and one draw needn't show every extreme that they name: `routes`: each row names 8 different experts, two in each of 4 different bases; at most 8 rows of one device route to one base, and some device has a base that 8 of its rows route to. `expert_map`: A permutation of the 64 slots.
All inputs are finite; a program needn't handle non-finite values. No bound on the sum of `row_counts` on one device may be relied on, other than what follows from the above.
Results may differ from a plain program's by a relative error of at most 0.015.
Values may be sent and summed in bfloat16 or wider, within the bound.
No kernel may reach another device: no remote copies, remote signals or barrier semaphores. Data moves between devices by JAX's collectives and lax.ppermute only.
A program may use at most 64 MiB of HBM per device.

v0:
```python
import jax
import jax.numpy as jnp
from jax import lax
from jax.sharding import PartitionSpec as P

JSLOT = 8
BTOP = 4


def slot_table(routes, gate_values, expert_map, live_mask):
    experts = expert_map.shape[0]
    identity_ids = jnp.arange(experts, dtype=jnp.int32)
    matches = routes[:, :, None] == identity_ids[None, None, :]
    slot_ids = jnp.sum(jnp.where(matches, expert_map[None, None, :], 0), axis=2)
    chosen = slot_ids[:, :, None] == identity_ids[None, None, :]
    spread = jnp.sum(
        jnp.where(chosen, gate_values.astype(jnp.float32)[:, :, None], jnp.float32(0.0)), axis=1
    )
    spread = jnp.where(live_mask[:, None], spread, jnp.float32(0.0))
    return spread.astype(jnp.bfloat16)


def placement_table(slot_gates, base_count, capacity):
    blocks, row_total, slot_count = slot_gates.shape
    grouped = slot_gates.reshape(blocks, row_total, base_count, slot_count // base_count)
    member = jnp.sum((grouped > 0).astype(jnp.int32), axis=3) > 0
    counted = member.astype(jnp.int32)
    before = jnp.cumsum(counted, axis=1) - counted
    target = jnp.where(member, before, -1)
    return (target[:, :, :, None] == jnp.arange(capacity, dtype=jnp.int32)).astype(jnp.bfloat16)


def slice_term(sent_rows, sent_gates, gate_part, up_part, down_part, in_part, out_part, first_slot):
    slot_span = in_part.shape[0]
    gate_value = jnp.dot(sent_rows, gate_part, preferred_element_type=jnp.float32)
    up_value = jnp.dot(sent_rows, up_part, preferred_element_type=jnp.float32)
    hidden = (jax.nn.silu(gate_value) * up_value).astype(jnp.bfloat16)
    shared = jnp.dot(hidden, down_part, preferred_element_type=jnp.float32)
    gate_total = jnp.sum(sent_gates.astype(jnp.float32), axis=1, keepdims=True)
    own_gates = lax.dynamic_slice_in_dim(sent_gates, first_slot, slot_span, 1).astype(jnp.float32)
    latent = jnp.einsum(
        "nd,jdr->jnr", sent_rows, in_part, preferred_element_type=jnp.float32
    ).astype(jnp.bfloat16)
    lifted = jnp.einsum("jnr,jrd->jnd", latent, out_part, preferred_element_type=jnp.float32)
    deltas = jnp.einsum("nj,jnd->nd", own_gates, lifted)
    return gate_total * shared + deltas


def body(
    tokens,
    routes,
    gate_values,
    expert_map,
    row_counts,
    gate_weight,
    up_weight,
    down_weight,
    delta_in,
    delta_out,
):
    row_total = tokens.shape[0]
    width = tokens.shape[1]
    dp_size = lax.axis_size("dp")
    expert_size = lax.axis_size("expert")
    slot_count = expert_map.shape[0]
    capacity = 2 * BTOP * row_total // expert_size
    live_mask = jnp.arange(row_total, dtype=jnp.int32) < row_counts[0]
    slot_gates = slot_table(routes, gate_values, expert_map, live_mask)
    own_placed = placement_table(slot_gates[None], expert_size, capacity)[0]
    all_tokens, all_gates = (
        lax.all_gather(tokens, "dp", axis=0, tiled=True),
        lax.all_gather(slot_gates, "dp", axis=0, tiled=True),
    )
    placed = placement_table(
        all_gates.reshape(dp_size, row_total, slot_count), expert_size, capacity
    )
    sent_rows = jnp.einsum(
        "nrbc,nrd->nbcd",
        placed,
        all_tokens.reshape(dp_size, row_total, width),
        preferred_element_type=jnp.float32,
    ).astype(jnp.bfloat16)
    sent_gates = jnp.einsum(
        "nrbc,nrbj->nbcj",
        placed,
        all_gates.reshape(dp_size, row_total, expert_size, JSLOT),
        preferred_element_type=jnp.float32,
    ).astype(jnp.bfloat16)
    got_rows, got_gates = (
        lax.all_to_all(sent_rows, "expert", split_axis=1, concat_axis=1, tiled=True),
        lax.all_to_all(sent_gates, "expert", split_axis=1, concat_axis=1, tiled=True),
    )
    flat_rows = got_rows.reshape(-1, width)
    flat_gates = got_gates.reshape(-1, JSLOT)
    slot_span = JSLOT // dp_size
    first_slot = lax.axis_index("dp") * slot_span
    gate_part = gate_weight[0]
    up_part = up_weight[0]
    down_part = down_weight[0]
    in_part = delta_in[0]
    out_part = delta_out[0]
    summed = lax.psum_scatter(
        slice_term(
            flat_rows, flat_gates, gate_part, up_part, down_part, in_part, out_part, first_slot
        ).astype(jnp.bfloat16),
        "dp",
        scatter_dimension=0,
        tiled=True,
    )
    results = lax.all_to_all(
        summed.reshape(expert_size, capacity, width),
        "expert",
        split_axis=0,
        concat_axis=0,
        tiled=True,
    )
    mixed = jnp.einsum("rbc,bcd->rd", own_placed, results, preferred_element_type=jnp.float32)
    return mixed.astype(jnp.bfloat16)


def solution(mesh):
    in_specs = (
        P(("dp", "expert"), None),
        P(("dp", "expert"), None),
        P(("dp", "expert"), None),
        P(),
        P(("dp", "expert")),
        P("expert", None, "dp"),
        P("expert", None, "dp"),
        P("expert", "dp", None),
        P("expert", "dp", None, None),
        P("expert", "dp", None, None),
    )
    out_specs = P(("dp", "expert"), None)
    return jax.shard_map(body, mesh=mesh, in_specs=in_specs, out_specs=out_specs, check_vma=False)
```

profile of v0, /device:TPU:0, one launch (start us, length us, event | category | flops | bytes accessed | tf_op | source)
XLA Modules:
  0.0 162.9 jit_solution(12481493179372716351)
XLA Ops:
  6.5 0.7 convert_element_type.85
  7.9 1.0 select_reduce_fusion.1
  8.9 0.1 select_reduce_fusion
  9.0 0.1 select_convert_fusion.1
  9.0 13.6 %all_gather.6 = bf16[32,64]{1,0:T(8,128)(2,1)S(1)} all-gather(bf16[8,64]{1,0:T(8,128)(2,1)S(1)} %select_convert_fusion.1), channel_id=1, replica_groups=mesh['dp'=4,'expert'=8] {'dp'}, dimensions={0}, use_global_device_ids=true | all-gather | bytes 5120 | tf_op jit(solution)/shard_map/all_gather | solution.py:72
  22.7 0.1 reshape_reshape.3
  22.8 0.6 convert_reduce_fusion.1
  23.5 0.1 copy.41
  23.5 0.2 convolution_convert_fusion.1
  23.7 0.7 reshape.106
  24.4 3.7 %all-to-all-start = ((bf16[8,2,128]{2,1,0:T(2,128)(2,1)}), bf16[8,2,128]{2,1,0:T(2,128)(2,1)S(1)}, u32[]{:S(2)}, u32[]{:S(2)}) async-start(bf16[8,2,128]{2,1,0:T(2,128)(2,1)} %reshape.106), calls=%async_computation | async-start | bytes 8192 | tf_op jit(solution)/shard_map/all_to_all | solution.py:91
  28.1 14.0 %all_gather.7 = bf16[32,3584]{1,0:T(8,128)(2,1)S(1)} all-gather(bf16[8,3584]{1,0:T(8,128)(2,1)} %param.10), channel_id=1, replica_groups=mesh['dp'=4,'expert'=8] {'dp'}, dimensions={0}, use_global_device_ids=true | all-gather | bytes 286720 | tf_op jit(solution)/shard_map/all_gather | solution.py:71
  42.2 0.6 convolution_convert_fusion
  42.8 1.4 copy.45
  44.2 0.0 all-to-all-done
  44.2 4.3 %all-to-all-start.1 = ((bf16[4,8,8,3584]{3,2,0,1:T(8,128)(2,1)}), bf16[4,8,8,3584]{3,2,0,1:T(8,128)(2,1)}, u32[]{:S(2)}, u32[]{:S(2)}) async-start(bf16[4,8,8,3584]{3,2,0,1:T(8,128)(2,1)} %copy.45), calls=%async_computation.1 | async-start | bytes 3670016 | tf_op jit(solution)/shard_map/all_to_all | solution.py:90
  48.5 0.0 reduce-scatter.2.cloned.1.call-start
  48.6 0.1 reshape.107
  48.7 0.2 copy.47
  48.8 0.1 reshape.99
  49.0 0.2 copy.49
  49.2 0.1 convert_reduce_fusion
  49.3 0.1 mul.20
  49.4 22.9 %all-to-all-done.1 = bf16[4,8,8,3584]{3,2,0,1:T(8,128)(2,1)} async-done(((bf16[4,8,8,3584]{3,2,0,1:T(8,128)(2,1)}), bf16[4,8,8,3584]{3,2,0,1:T(8,128)(2,1)}, u32[]{:S(2)}, u32[]{:S(2)}) %all-to-all-start.1) | async-done | bytes 1835040 | tf_op jit(solution)/shard_map/all_to_all | solution.py:90
  72.3 1.6 %copy.46 = bf16[4,8,8,3584]{3,2,1,0:T(8,128)(2,1)S(1)} copy(bf16[4,8,8,3584]{3,2,0,1:T(8,128)(2,1)} %all-to-all-done.1) | data formatting | bytes 3670016 | tf_op jit(solution)/shard_map/all_to_all | solution.py:90
  74.0 7.1 %fusion.5 = bf16[2,256,3584]{2,1,0:T(8,128)(2,1)} fusion(bf16[1,2,256,3584]{3,2,1,0:T(8,128)(2,1)} %param.19, bf16[256,3584,1]{1,0,2:T(8,128)(2,1)S(1)} %bitcast.66, bf16[1,2,3584,256]{3,2,1,0:T(8,128)(2,1)} %param.18), kind=kOutput, calls=%fused_computation.8 | convolution fusion | flops 1879179264 | bytes 12845056 | tf_op jit(solution)/shard_map/jnr,jrd->jnd/dot_general | solution.py:44
  81.1 0.0 copy-start
  81.1 14.9 %fusion = f32[256,1,3584]{2,1,0:T(1,128)} fusion(bf16[256,2,1]{1,2,0:T(2,128)(2,1)S(1)} %copy.49, bf16[2,256,3584]{2,1,0:T(8,128)(2,1)} %fusion.5), kind=kOutput, calls=%fused_computation | convolution fusion | flops 3670016 | bytes 7341056 | tf_op jit(solution)/shard_map/nj,jnd->nd/dot_general | solution.py:45
  96.0 0.0 copy-done
  96.0 1.1 fusion.12
  97.1 7.6 %fusion.3 = bf16[256,3584]{1,0:T(8,128)(2,1)} fusion(bf16[1,512,3584]{2,1,0:T(8,128)(2,1)} %param.17, f32[256,1,3584]{2,1,0:T(1,128)} %fusion, f32[256]{0:T(256)S(1)} %mul.20, bf16[256,3584]{1,0:T(8,128)(2,1)S(1)} %bitcast.68, bf16[1,3584,512]{2,1,0:T(8,128)(2,1)} %param.16, f32[256,512]{1,0:T(8,128)S(1)} %fusion.12), kind=kOutput, calls=%fused_computation.4 | convolution fusion | flops 1882587136 | bytes 15205376 | tf_op jit(solution)/shard_map/dot_general | solution.py:38
  104.7 0.0 reduce-scatter.2.cloned.1.call-update
  104.8 0.1 reduce_sum.49
  104.8 0.3 convert_reduce_fusion.2
  105.1 37.3 %reduce-scatter.2.cloned.1.call-done = bf16[64,3584]{1,0:T(8,128)(2,1)} async-done(((bf16[256,3584]{1,0:T(8,128)(2,1)}), bf16[64,3584]{1,0:T(8,128)(2,1)}) %reduce-scatter.2.cloned.1.call-update) | async-done | bytes 458768 | tf_op jit(solution)/shard_map/reduce_scatter | solution.py:102
  142.4 3.6 %all-to-all-start.2 = ((bf16[8,8,3584]{2,1,0:T(8,128)(2,1)}), bf16[8,8,3584]{2,1,0:T(8,128)(2,1)S(1)}, u32[]{:S(2)}, u32[]{:S(2)}) async-start(bf16[8,8,3584]{2,1,0:T(8,128)(2,1)} %bitcast.70), calls=%async_computation.3 | async-start | bytes 917504 | tf_op jit(solution)/shard_map/all_to_all | solution.py:110
  146.1 0.1 copy.40
  146.2 8.9 %all-to-all-done.2 = bf16[8,8,3584]{2,1,0:T(8,128)(2,1)S(1)} async-done(((bf16[8,8,3584]{2,1,0:T(8,128)(2,1)}), bf16[8,8,3584]{2,1,0:T(8,128)(2,1)S(1)}, u32[]{:S(2)}, u32[]{:S(2)}) %all-to-all-start.2) | async-done | bytes 458784 | tf_op jit(solution)/shard_map/all_to_all | solution.py:110
  155.0 1.0 fusion.4
  (10 shorter events, 0.1 us)
Async XLA Ops:
  24.4 19.8 %all-to-all-start = ((bf16[8,2,128]{2,1,0:T(2,128)(2,1)}), bf16[8,2,128]{2,1,0:T(2,128)(2,1)S(1)}, u32[]{:S(2)}, u32[]{:S(2)}) async-start(bf16[8,2,128]{2,1,0:T(2,128)(2,1)} %reshape.106), calls=%async_computation | async-start | bytes 8192 | tf_op jit(solution)/shard_map/all_to_all | solution.py:91
  44.2 28.1 %all-to-all-start.1 = ((bf16[4,8,8,3584]{3,2,0,1:T(8,128)(2,1)}), bf16[4,8,8,3584]{3,2,0,1:T(8,128)(2,1)}, u32[]{:S(2)}, u32[]{:S(2)}) async-start(bf16[4,8,8,3584]{3,2,0,1:T(8,128)(2,1)} %copy.45), calls=%async_computation.1 | async-start | bytes 3670016 | tf_op jit(solution)/shard_map/all_to_all | solution.py:90
  48.5 93.9 %reduce-scatter.2.cloned.1.call-start = ((), (), s32[]{:S(2)}) async-start(), calls=%async_computation.4 | async-start | bytes 2293760 | tf_op jit(solution)/shard_map/reduce_scatter | solution.py:102
  81.1 14.9 %copy-start = (bf16[1,3584,512]{2,1,0:T(8,128)(2,1)S(1)}, bf16[1,3584,512]{2,1,0:T(8,128)(2,1)}, u32[]{:S(2)}) copy-start(bf16[1,3584,512]{2,1,0:T(8,128)(2,1)} %param.15) | copy-start | bytes 11010052
  142.4 12.6 %all-to-all-start.2 = ((bf16[8,8,3584]{2,1,0:T(8,128)(2,1)}), bf16[8,8,3584]{2,1,0:T(8,128)(2,1)S(1)}, u32[]{:S(2)}, u32[]{:S(2)}) async-start(bf16[8,8,3584]{2,1,0:T(8,128)(2,1)} %bitcast.70), calls=%async_computation.3 | async-start | bytes 917504 | tf_op jit(solution)/shard_map/all_to_all | solution.py:110
Sparse Core Ops, SparseCore 0:
  104.9 37.4 reduce-scatter.1
where the time goes:
time: 163 us
  waiting for transfers between devices  69.1 us (42%)
  matrix products  32.6 us (20%)
  blocking collectives  27.7 us (17%)
  between operations  14.2 us (9%)
  starting transfers between devices  11.7 us (7%)
  local copies, waits for them, and re-layouts  4.78 us (3%)
  other arithmetic  2.95 us (2%)
    reduce_scatter x1, waiting for transfers between devices, body(): lax.psum_scatter(slice_term(flat_rows, flat_gates, gate_part, up_part, do...  37.3 us
    all_to_all x1, waiting for transfers between devices, body(): lax.all_to_all(sent_rows, 'expert', split_axis=1, concat_axis=1, tiled=True)  22.9 us
    dot_general x1, matrix products, slice_term(): deltas = jnp.einsum('nj,jnd->nd', own_gates, lifted)  14.9 us
    all_gather x1, blocking collectives, body(): lax.all_gather(tokens, 'dp', axis=0, tiled=True)  14 us
    all_gather x1, blocking collectives, body(): lax.all_gather(slot_gates, 'dp', axis=0, tiled=True)  13.6 us
    all_to_all x1, waiting for transfers between devices, body(): lax.all_to_all(summed.reshape(expert_size, capacity, width), 'expert', sp...  8.9 us
    dot_general x1, matrix products, slice_term(): shared = jnp.dot(hidden, down_part, preferred_element_type=jnp.float32)  7.62 us
    dot_general x1, matrix products, slice_term(): jnp.einsum('jnr,jrd->jnd', latent, out_part, preferred_element_type=jnp.f...  7.14 us
  transfers between devices with their start and end apart: 4, of which 3 were waited for; matrix products, arithmetic and copies ran while one was open for 2% of the time, Pallas kernels for 0%

commit v1 on v0

--- a/solution.py
+++ b/solution.py
@@ -1,6 +1,10 @@
+import functools
+
 import jax
 import jax.numpy as jnp
 from jax import lax
+from jax.experimental import pallas as pl
+from jax.experimental.pallas import tpu as pltpu
 from jax.sharding import PartitionSpec as P
 
 JSLOT = 8
@@ -117,6 +121,174 @@
     mixed = jnp.einsum("rbc,bcd->rd", own_placed, results, preferred_element_type=jnp.float32)
     return mixed.astype(jnp.bfloat16)
 
+AXES = ("dp", "expert")
+LANES = 128
+TILE = 256
+CORES = 2
+
+
+def exchange(value, dp_size, expert_size, dp_bits, expert_bits):
+    pairs = [
+        (z * expert_size + e, (z ^ dp_bits) * expert_size + (e ^ expert_bits))
+        for z in range(dp_size)
+        for e in range(expert_size)
+    ]
+    return lax.ppermute(value, AXES, pairs)
+
+
+def ffn_kernel(pieces, ids, *refs):
+    rows_in, refs = refs[:pieces], refs[pieces:]
+    gate_w, up_w, down_w, in_w, out_w = refs[:5]
+    outs, (rows, act, scale) = refs[5 : 5 + pieces], refs[5 + pieces :]
+    count = rows_in[0].shape[0]
+    width, hidden = gate_w.shape
+    span, _, rank = in_w.shape
+    top = ids.shape[0]
+    for p in range(pieces):
+        here = slice(p * count, (p + 1) * count)
+        rows[here] = rows_in[p][:, :width]
+        meta = rows_in[p][:, width:].astype(jnp.float32)
+        values = pltpu.roll(meta, LANES - top, 1)
+        lane = lax.broadcasted_iota(jnp.int32, meta.shape, 1)
+        total = jnp.zeros_like(meta)
+        for j in range(JSLOT):
+            picked = jnp.where((meta == ids[j]) & (lane < top), values, 0.0)
+            total += picked
+            if j < span:
+                scale[j, here] = jnp.broadcast_to(
+                    jnp.sum(picked, axis=1, keepdims=True), meta.shape
+                )
+        scale[span, here] = jnp.broadcast_to(jnp.sum(total, axis=1, keepdims=True), meta.shape)
+
+    def wide(j, columns):
+        return jnp.concatenate([scale[j]] * (columns // LANES), axis=1)
+
+    @pl.loop(0, hidden // TILE)
+    def _(i):
+        cols = pl.ds(pl.multiple_of(i * TILE, TILE), TILE)
+        gate = jnp.dot(rows[...], gate_w[:, cols], preferred_element_type=jnp.float32)
+        up = jnp.dot(rows[...], up_w[:, cols], preferred_element_type=jnp.float32)
+        value = gate / (1.0 + jnp.exp(-gate)) * up * wide(span, TILE)
+        act[:, cols] = value.astype(jnp.bfloat16)
+
+    @pl.loop(0, span)
+    def _(j):
+        latent = jnp.dot(rows[...], in_w[j], preferred_element_type=jnp.float32)
+        cols = pl.ds(pl.multiple_of(hidden + j * rank, LANES), rank)
+        act[:, cols] = (latent * wide(j, rank)).astype(jnp.bfloat16)
+
+    @pl.loop(0, width // TILE)
+    def _(i):
+        cols = pl.ds(pl.multiple_of(i * TILE, TILE), TILE)
+        value = jnp.dot(act[:, :hidden], down_w[:, cols], preferred_element_type=jnp.float32)
+        for j in range(span):
+            low = hidden + j * rank
+            value += jnp.dot(
+                act[:, low : low + rank], out_w[j, :, cols], preferred_element_type=jnp.float32
+            )
+        value = value.astype(jnp.bfloat16)
+        for p in range(pieces):
+            outs[p][:, cols] = value[p * count : (p + 1) * count]
+
+
+def ffn(ids, rows_in, weights):
+    pieces = len(rows_in)
+    count = rows_in[0].shape[0]
+    width, hidden = weights[0].shape
+    span, _, rank = weights[3].shape
+    total = pieces * count
+    inner = hidden + span * rank
+    vmem = pl.BlockSpec(memory_space=pltpu.VMEM)
+    weights = [pltpu.with_memory_space_constraint(w, pltpu.VMEM) for w in weights]
+    return pl.pallas_call(
+        functools.partial(ffn_kernel, pieces),
+        out_shape=[jax.ShapeDtypeStruct((count, width), jnp.bfloat16)] * pieces,
+        in_specs=[pl.BlockSpec(memory_space=pltpu.SMEM)] + [vmem] * (pieces + 5),
+        out_specs=[vmem] * pieces,
+        scratch_shapes=[
+            pltpu.VMEM((total, width), jnp.bfloat16),
+            pltpu.VMEM((total, inner), jnp.bfloat16),
+            pltpu.VMEM((span + 1, total, LANES), jnp.float32),
+        ],
+        compiler_params=pltpu.CompilerParams(vmem_limit_bytes=16 << 20),
+        cost_estimate=pl.CostEstimate(
+            flops=2 * total * width * (2 * hidden + span * rank + inner),
+            bytes_accessed=2 * width * (2 * hidden + span * rank + inner + 2 * total),
+            transcendentals=total * hidden,
+        ),
+    )(ids, *rows_in, *weights)
+
+
+def add(*terms):
+    return sum(term.astype(jnp.float32) for term in terms)
+
+
+def dense_body(
+    tokens,
+    routes,
+    gate_values,
+    expert_map,
+    row_counts,
+    gate_weight,
+    up_weight,
+    down_weight,
+    delta_in,
+    delta_out,
+):
+    row_total = tokens.shape[0]
+    top = routes.shape[1]
+    dp_size = lax.axis_size("dp")
+    expert_size = lax.axis_size("expert")
+    chips = expert_size // CORES
+    slot_span = JSLOT // dp_size
+
+    def swap(value, dp_bits=0, chip_bits=0, core_bits=0):
+        return exchange(value, dp_size, expert_size, dp_bits, chip_bits * CORES + core_bits)
+
+    live = jnp.arange(row_total, dtype=jnp.int32) < row_counts[0]
+    message = jnp.concatenate(
+        [
+            tokens,
+            routes.astype(jnp.bfloat16),
+            jnp.where(live[:, None], gate_values, jnp.bfloat16(0.0)),
+            jnp.zeros((row_total, LANES - 2 * top), jnp.bfloat16),
+        ],
+        axis=1,
+    )
+    column = jnp.concatenate(
+        [message] + [swap(message, dp_bits=k) for k in range(1, dp_size)], axis=0
+    )
+    mine = [column] + [swap(column, chip_bits=k) for k in range(1, chips)]
+    theirs = [swap(piece, core_bits=1) for piece in mine]
+
+    first = lax.axis_index("expert") * JSLOT
+    shift = lax.axis_index("dp") * slot_span
+    slots = first + (shift + jnp.arange(JSLOT, dtype=jnp.int32)) % JSLOT
+    experts = jnp.arange(expert_map.shape[0], dtype=jnp.int32)
+    ids = jnp.sum(jnp.where(expert_map[None, :] == slots[:, None], experts[None, :], 0), axis=1)
+    weights = [gate_weight[0], up_weight[0], down_weight[0], delta_in[0], delta_out[0]]
+    partial = ffn(ids.astype(jnp.float32), mine + theirs, weights)
+
+    kept, given = partial[:chips], partial[chips:]
+    paired = [
+        add(own, swap(other, core_bits=1)).astype(jnp.bfloat16) for own, other in zip(kept, given)
+    ]
+    summed = add(paired[0], *[swap(paired[k], chip_bits=k) for k in range(1, chips)])
+    summed = summed.astype(jnp.bfloat16)
+    blocks = [summed[k * row_total : (k + 1) * row_total] for k in range(dp_size)]
+    mixed = add(blocks[0], *[swap(blocks[k], dp_bits=k) for k in range(1, dp_size)])
+    return mixed.astype(jnp.bfloat16)
+
+
+def power_of_two(n):
+    return n & (n - 1) == 0
+
+
+def serves_all_rows(mesh):
+    dp_size, expert_size = mesh.shape["dp"], mesh.shape["expert"]
+    shaped = power_of_two(dp_size) and power_of_two(expert_size) and expert_size >= CORES
+    return shaped and JSLOT % dp_size == 0 and 2 * BTOP >= expert_size
+
 
 def solution(mesh):
     in_specs = (
@@ -132,4 +304,5 @@
         P("expert", "dp", None, None),
     )
     out_specs = P(("dp", "expert"), None)
-    return jax.shard_map(body, mesh=mesh, in_specs=in_specs, out_specs=out_specs, check_vma=False)
+    chosen = dense_body if serves_all_rows(mesh) else body
+    return jax.shard_map(chosen, mesh=mesh, in_specs=in_specs, out_specs=out_specs, check_vma=False)

time: 163 us -> 72.5 us (0.44)
  waiting for transfers between devices: 69.1 us -> 30 us
  matrix products: 32.6 us -> 0 us
  blocking collectives: 27.7 us -> 0 us
  between operations: 14.2 us -> 0.73 us
  Pallas kernels: 0 us -> 8.97 us
  local copies, waits for them, and re-layouts: 4.78 us -> 11.1 us
  starting transfers between devices: 11.7 us -> 18 us
    reduce_scatter x1 -> x0, waiting for transfers between devices: 37.3 us -> none  [body(): lax.psum_scatter(slice_term(flat_rows, flat_gates, gate_part, up_part, do...]
    dot_general x7 -> x0, matrix products: 32.6 us -> none  [the longest x1 14.9 us: slice_term(): deltas = jnp.einsum('nj,jnd->nd', own_gates, lifted)]
    all_to_all x3 -> x0, waiting for transfers between devices: 31.8 us -> none  [the longest x1 22.9 us: body(): lax.all_to_all(sent_rows, 'expert', split_axis=1, concat_axis=1, tiled=True)]
    ppermute x0 -> x20, waiting for transfers between devices: none -> 30 us  [exchange(): return lax.ppermute(value, AXES, pairs)]
    all_gather x2 -> x0, blocking collectives: 27.7 us -> none  [the longest x1 14 us: body(): lax.all_gather(tokens, 'dp', axis=0, tiled=True)]
    ppermute x0 -> x20, starting transfers between devices: none -> 18 us  [exchange(): return lax.ppermute(value, AXES, pairs)]
    all_to_all x3 -> x0, starting transfers between devices: 11.7 us -> none  [the longest x1 4.31 us: body(): lax.all_to_all(sent_rows, 'expert', split_axis=1, concat_axis=1, tiled=True)]
    unnamed x4 -> x10, local copies, waits for them, and re-layouts: 0.83 us -> 10.2 us
  transfers between devices with their start and end apart: 4 -> 20, of which waited for: 3 -> 13; matrix products, arithmetic and copies ran while one was open for 2% -> 1% of each run, Pallas kernels for 0% -> 0%
where the time goes in v1:
time: 72.5 us; the launch traced here: 72.1 us
  waiting for transfers between devices  30 us (41%)
  starting transfers between devices  18 us (25%)
  local copies, waits for them, and re-layouts  11.1 us (15%)
  Pallas kernels  8.97 us (12%)
  other arithmetic  3.3 us (5%)
  between operations  0.73 us (1%)
    ppermute x20, waiting for transfers between devices, exchange(): return lax.ppermute(value, AXES, pairs)  30 us
    ppermute x20, starting transfers between devices, exchange(): return lax.ppermute(value, AXES, pairs)  18 us
    unnamed x10, local copies, waits for them, and re-layouts  10.2 us
    pallas_call x1, Pallas kernels, ffn(): pl.pallas_call(functools.partial(ffn_kernel, pieces), out_shape=[jax.Shap...  8.97 us
  transfers between devices with their start and end apart: 20, of which 13 were waited for; matrix products, arithmetic and copies ran while one was open for 1% of the time, Pallas kernels for 0%

profile of v1, /device:TPU:0, one launch (start us, length us, event | category | flops | bytes accessed | tf_op | source)
XLA Modules:
  0.0 72.1 jit_solution(15349154482414703488)
XLA Ops:
  0.7 0.7 convert_element_type.73
  1.4 0.8 %broadcast_select_fusion = bf16[8,8]{1,0:T(8,128)(2,1)S(1)} fusion(bf16[8,8]{1,0:T(8,128)(2,1)} %param.12, pred[8]{0:T(512)(128)(4,1)S(1)} %iota_compare_fusion), kind=kLoop, calls=%fused_computation.10 | loop fusion | flops 64 | bytes 264 | tf_op jit(solution)/shard_map/jit(_where)/select_n | solution.py:253
  2.1 0.9 %concatenate.6 = bf16[8,3712]{1,0:T(8,128)(2,1)S(1)} concatenate(bf16[8,3584]{1,0:T(8,128)(2,1)} %param.10, bf16[8,8]{1,0:T(8,128)(2,1)S(1)} %convert_element_type.73, bf16[8,8]{1,0:T(8,128)(2,1)S(1)} %broadcast_select_fusion, bf16[8,112]{1,0:T(8,128)(2,1)S(1)} %broadcast_in_dim.35), dimensions={1} | concatenate | bytes 118784 | tf_op jit(solution)/shard_map/concatenate | solution.py:249
  3.0 5.1 %collective-permute-start.2 = (bf16[8,3712]{1,0:T(8,128)(2,1)S(1)}, bf16[8,3712]{1,0:T(8,128)(2,1)S(1)}, u32[]{:S(2)}, u32[]{:S(2)}) collective-permute-start(bf16[8,3712]{1,0:T(8,128)(2,1)S(1)} %concatenate.6), channel_id=1, source_target_pairs={{0,24},{1,25},{2,26},{3,27},{4,28},{5,29},{6,30},{7,31},{8,16},{9,... | collective-permute-start | bytes 178184 | tf_op jit(solution)/shard_map/ppermute | solution.py:136
  8.1 0.0 collective-permute-start.1
  8.1 0.6 collective-permute-start
  8.7 1.7 %collective-permute-done.2 = bf16[8,3712]{1,0:T(8,128)(2,1)S(1)} collective-permute-done((bf16[8,3712]{1,0:T(8,128)(2,1)S(1)}, bf16[8,3712]{1,0:T(8,128)(2,1)S(1)}, u32[]{:S(2)}, u32[]{:S(2)}) %collective-permute-start.2) | collective-permute-done | bytes 59424 | tf_op jit(solution)/shard_map/ppermute | solution.py:136
  10.4 2.8 %collective-permute-done.1 = bf16[8,3712]{1,0:T(8,128)(2,1)S(1)} collective-permute-done((bf16[8,3712]{1,0:T(8,128)(2,1)S(1)}, bf16[8,3712]{1,0:T(8,128)(2,1)S(1)}, u32[]{:S(2)}, u32[]{:S(2)}) %collective-permute-start.1) | collective-permute-done | bytes 59424 | tf_op jit(solution)/shard_map/ppermute | solution.py:136
  13.3 2.6 %collective-permute-start.5 = (bf16[32,3712]{1,0:T(8,128)(2,1)S(1)}, bf16[32,3712]{1,0:T(8,128)(2,1)S(1)}, u32[]{:S(2)}, u32[]{:S(2)}) collective-permute-start(bf16[32,3712]{1,0:T(8,128)(2,1)S(1)} %pad_maximum_fusion.refs_0_), channel_id=1, source_target_pairs={{0,6},{1,7},{2,4},{3,5},{4,2},{5,3},{6,0},{7,1},{8,14},{9,15},{10,... | collective-permute-start | bytes 712712 | tf_op jit(solution)/shard_map/ppermute | solution.py:136
  15.9 0.5 collective-permute-start.4
  16.4 0.4 collective-permute-start.3
  16.8 6.1 %collective-permute-done.5.refs_3_ = bf16[32,3712]{1,0:T(8,128)(2,1)S(1)} collective-permute-done((bf16[32,3712]{1,0:T(8,128)(2,1)S(1)}, bf16[32,3712]{1,0:T(8,128)(2,1)S(1)}, u32[]{:S(2)}, u32[]{:S(2)}) %collective-permute-start.5) | collective-permute-done | bytes 237600 | tf_op jit(solution)/shard_map/ppermute | solution.py:136
  22.9 0.0 collective-permute-start.9
  23.0 3.6 %collective-permute-done.4.refs_2_ = bf16[32,3712]{1,0:T(8,128)(2,1)S(1)} collective-permute-done((bf16[32,3712]{1,0:T(8,128)(2,1)S(1)}, bf16[32,3712]{1,0:T(8,128)(2,1)S(1)}, u32[]{:S(2)}, u32[]{:S(2)}) %collective-permute-start.4) | collective-permute-done | bytes 237600 | tf_op jit(solution)/shard_map/ppermute | solution.py:136
  26.5 0.0 collective-permute-start.8
  26.5 0.1 collective-permute-done.3.refs_1_
  26.6 0.4 collective-permute-start.7
  27.1 0.8 %select_reduce_fusion = s32[8]{0:T(128)S(1)} fusion(s32[64]{0:T(128)} %param.13, s32[8]{0:T(128)S(1)} %fusion), kind=kLoop, calls=%fused_computation.7 | loop fusion | flops 1528 | bytes 320 | tf_op jit(solution)/shard_map/reduce_sum | solution.py:268
  27.9 0.0 collective-permute-done.9.refs_7_
  27.9 0.1 collective-permute-done.8.refs_6_
  28.0 0.3 collective-permute-done.7.refs_5_
  28.4 2.0 %copy-done = bf16[1,3584,512]{2,1,0:T(8,128)(2,1)S(1)} copy-done((bf16[1,3584,512]{2,1,0:T(8,128)(2,1)S(1)}, bf16[1,3584,512]{2,1,0:T(8,128)(2,1)}, u32[]{:S(2)}) %copy-start) | copy-done | bytes 3670040
  30.4 2.0 %copy-done.1 = bf16[1,3584,512]{2,1,0:T(8,128)(2,1)S(1)} copy-done((bf16[1,3584,512]{2,1,0:T(8,128)(2,1)S(1)}, bf16[1,3584,512]{2,1,0:T(8,128)(2,1)}, u32[]{:S(2)}) %copy-start.1) | copy-done | bytes 3670040
  32.4 2.0 %copy-done.2 = bf16[1,512,3584]{2,1,0:T(8,128)(2,1)S(1)} copy-done((bf16[1,512,3584]{2,1,0:T(8,128)(2,1)S(1)}, bf16[1,512,3584]{2,1,0:T(8,128)(2,1)}, u32[]{:S(2)}) %copy-start.2) | copy-done | bytes 3670040
  34.5 2.0 %copy-done.3 = bf16[1,2,3584,256]{3,2,1,0:T(8,128)(2,1)S(1)} copy-done((bf16[1,2,3584,256]{3,2,1,0:T(8,128)(2,1)S(1)}, bf16[1,2,3584,256]{3,2,1,0:T(8,128)(2,1)}, u32[]{:S(2)}) %copy-start.3) | copy-done | bytes 3670040
  36.5 2.0 %copy-done.4 = bf16[1,2,256,3584]{3,2,1,0:T(8,128)(2,1)S(1)} copy-done((bf16[1,2,256,3584]{3,2,1,0:T(8,128)(2,1)S(1)}, bf16[1,2,256,3584]{3,2,1,0:T(8,128)(2,1)}, u32[]{:S(2)}) %copy-start.4) | copy-done | bytes 3670040
  38.6 9.0 %shard_map.100 = (bf16[32,3584]{1,0:T(8,128)(2,1)S(1)}, bf16[32,3584]{1,0:T(8,128)(2,1)S(1)}, bf16[32,3584]{1,0:T(8,128)(2,1)S(1)}, bf16[32,3584]{1,0:T(8,128)(2...) custom-call(f32[8]{0:T(128)S(1)} %convert_element_type.72.ids, ...), custom_call_target="tpu_custom_call" | custom-call | flops 4697620480 | bytes 22020096 | tf_op jit(solution)/shard_map/pallas_call | solution.py:203
  47.5 0.2 collective-permute-start.11
  47.8 0.3 collective-permute-start.10
  48.1 0.2 collective-permute-start.13
  48.3 0.3 collective-permute-start.15
  48.6 0.5 collective-permute-done.11
  49.1 0.1 add_convert_fusion.3
  49.2 1.6 %collective-permute-start.12 = (bf16[32,3584]{1,0:T(8,128)(2,1)S(1)}, bf16[32,3584]{1,0:T(8,128)(2,1)S(1)}, u32[]{:S(2)}, u32[]{:S(2)}) collective-permute-start(bf16[32,3584]{1,0:T(8,128)(2,1)S(1)} %add_convert_fusion.3), channel_id=1, source_target_pairs={{0,2},{1,3},{2,0},{3,1},{4,6},{5,7},{6,4},{7,5},{8,10},{9,11},{10,... | collective-permute-start | bytes 688136 | tf_op jit(solution)/shard_map/ppermute | solution.py:136
  50.7 0.1 add_convert_fusion.2
  50.8 0.9 %collective-permute-start.14 = (bf16[32,3584]{1,0:T(8,128)(2,1)S(1)}, bf16[32,3584]{1,0:T(8,128)(2,1)S(1)}, u32[]{:S(2)}, u32[]{:S(2)}) collective-permute-start(bf16[32,3584]{1,0:T(8,128)(2,1)S(1)} %add_convert_fusion.2), channel_id=1, source_target_pairs={{0,4},{1,5},{2,6},{3,7},{4,0},{5,1},{6,2},{7,3},{8,12},{9,13},{10,... | collective-permute-start | bytes 688136 | tf_op jit(solution)/shard_map/ppermute | solution.py:136
  51.7 0.1 add_convert_fusion.1
  51.7 1.2 %collective-permute-start.16 = (bf16[32,3584]{1,0:T(8,128)(2,1)S(1)}, bf16[32,3584]{1,0:T(8,128)(2,1)S(1)}, u32[]{:S(2)}, u32[]{:S(2)}) collective-permute-start(bf16[32,3584]{1,0:T(8,128)(2,1)S(1)} %add_convert_fusion.1), channel_id=1, source_target_pairs={{0,6},{1,7},{2,4},{3,5},{4,2},{5,3},{6,0},{7,1},{8,14},{9,15},{10,... | collective-permute-start | bytes 688136 | tf_op jit(solution)/shard_map/ppermute | solution.py:136
  53.0 4.7 %collective-permute-done.12 = bf16[32,3584]{1,0:T(8,128)(2,1)S(1)} collective-permute-done((bf16[32,3584]{1,0:T(8,128)(2,1)S(1)}, bf16[32,3584]{1,0:T(8,128)(2,1)S(1)}, u32[]{:S(2)}, u32[]{:S(2)}) %collective-permute-start.12) | collective-permute-done | bytes 229408 | tf_op jit(solution)/shard_map/ppermute | solution.py:136
  57.7 5.5 %collective-permute-done.14 = bf16[32,3584]{1,0:T(8,128)(2,1)S(1)} collective-permute-done((bf16[32,3584]{1,0:T(8,128)(2,1)S(1)}, bf16[32,3584]{1,0:T(8,128)(2,1)S(1)}, u32[]{:S(2)}, u32[]{:S(2)}) %collective-permute-start.14) | collective-permute-done | bytes 229408 | tf_op jit(solution)/shard_map/ppermute | solution.py:136
  63.2 0.1 add_convert_fusion
  63.3 0.4 collective-permute-start.17
  63.8 2.0 %collective-permute-start.19 = (bf16[8,3584]{1,0:T(8,128)(2,1)S(1)}, bf16[8,3584]{1,0:T(8,128)(2,1)S(1)}, u32[]{:S(2)}, u32[]{:S(2)}) collective-permute-start(bf16[8,3584]{1,0:T(8,128)(2,1)S(1)} %get-tuple-element.22), channel_id=1, source_target_pairs={{0,24},{1,25},{2,26},{3,27},{4,28},{5,29},{6,30},{7,31},{8,16},{9,... | collective-permute-start | bytes 172040 | tf_op jit(solution)/shard_map/ppermute | solution.py:136
  65.7 1.1 %collective-permute-start.18 = (bf16[8,3584]{1,0:T(8,128)(2,1)S(1)}, bf16[8,3584]{1,0:T(8,128)(2,1)S(1)}, u32[]{:S(2)}, u32[]{:S(2)}) collective-permute-start(bf16[8,3584]{1,0:T(8,128)(2,1)S(1)} %get-tuple-element.23), channel_id=1, source_target_pairs={{0,16},{1,17},{2,18},{3,19},{4,20},{5,21},{6,22},{7,23},{8,24},{9,... | collective-permute-start | bytes 172040 | tf_op jit(solution)/shard_map/ppermute | solution.py:136
  66.9 1.7 %collective-permute-done.17 = bf16[8,3584]{1,0:T(8,128)(2,1)S(1)} collective-permute-done((bf16[8,3584]{1,0:T(8,128)(2,1)S(1)}, bf16[8,3584]{1,0:T(8,128)(2,1)S(1)}, u32[]{:S(2)}, u32[]{:S(2)}) %collective-permute-start.17) | collective-permute-done | bytes 57376 | tf_op jit(solution)/shard_map/ppermute | solution.py:136
  68.6 1.2 %collective-permute-done.19 = bf16[8,3584]{1,0:T(8,128)(2,1)S(1)} collective-permute-done((bf16[8,3584]{1,0:T(8,128)(2,1)S(1)}, bf16[8,3584]{1,0:T(8,128)(2,1)S(1)}, u32[]{:S(2)}, u32[]{:S(2)}) %collective-permute-start.19) | collective-permute-done | bytes 57376 | tf_op jit(solution)/shard_map/ppermute | solution.py:136
  69.7 1.7 %collective-permute-done.18 = bf16[8,3584]{1,0:T(8,128)(2,1)S(1)} collective-permute-done((bf16[8,3584]{1,0:T(8,128)(2,1)S(1)}, bf16[8,3584]{1,0:T(8,128)(2,1)S(1)}, u32[]{:S(2)}, u32[]{:S(2)}) %collective-permute-start.18) | collective-permute-done | bytes 57376 | tf_op jit(solution)/shard_map/ppermute | solution.py:136
  71.4 0.7 add_convert_fusion.5
  (18 shorter events, 0.1 us)
Async XLA Ops:
  3.0 7.4 %collective-permute-start.2 = (bf16[8,3712]{1,0:T(8,128)(2,1)S(1)}, bf16[8,3712]{1,0:T(8,128)(2,1)S(1)}, u32[]{:S(2)}, u32[]{:S(2)}) collective-permute-start(bf16[8,3712]{1,0:T(8,128)(2,1)S(1)} %concatenate.6), channel_id=1, source_target_pairs={{0,24},{1,25},{2,26},{3,27},{4,28},{5,29},{6,30},{7,31},{8,16},{9,... | collective-permute-start | bytes 178184 | tf_op jit(solution)/shard_map/ppermute | solution.py:136
  8.1 5.2 %collective-permute-start.1 = (bf16[8,3712]{1,0:T(8,128)(2,1)S(1)}, bf16[8,3712]{1,0:T(8,128)(2,1)S(1)}, u32[]{:S(2)}, u32[]{:S(2)}) collective-permute-start(bf16[8,3712]{1,0:T(8,128)(2,1)S(1)} %concatenate.6), channel_id=1, source_target_pairs={{0,16},{1,17},{2,18},{3,19},{4,20},{5,21},{6,22},{7,23},{8,24},{9,... | collective-permute-start | bytes 178184 | tf_op jit(solution)/shard_map/ppermute | solution.py:136
  8.1 5.2 %collective-permute-start = (bf16[8,3712]{1,0:T(8,128)(2,1)S(1)}, bf16[8,3712]{1,0:T(8,128)(2,1)S(1)}, u32[]{:S(2)}, u32[]{:S(2)}) collective-permute-start(bf16[8,3712]{1,0:T(8,128)(2,1)S(1)} %concatenate.6), channel_id=1, source_target_pairs={{0,8},{1,9},{2,10},{3,11},{4,12},{5,13},{6,14},{7,15},{8,0},{9,1},... | collective-permute-start | bytes 178184 | tf_op jit(solution)/shard_map/ppermute | solution.py:136
  13.3 9.7 %collective-permute-start.5 = (bf16[32,3712]{1,0:T(8,128)(2,1)S(1)}, bf16[32,3712]{1,0:T(8,128)(2,1)S(1)}, u32[]{:S(2)}, u32[]{:S(2)}) collective-permute-start(bf16[32,3712]{1,0:T(8,128)(2,1)S(1)} %pad_maximum_fusion.refs_0_), channel_id=1, source_target_pairs={{0,6},{1,7},{2,4},{3,5},{4,2},{5,3},{6,0},{7,1},{8,14},{9,15},{10,... | collective-permute-start | bytes 712712 | tf_op jit(solution)/shard_map/ppermute | solution.py:136
  15.9 10.6 %collective-permute-start.4 = (bf16[32,3712]{1,0:T(8,128)(2,1)S(1)}, bf16[32,3712]{1,0:T(8,128)(2,1)S(1)}, u32[]{:S(2)}, u32[]{:S(2)}) collective-permute-start(bf16[32,3712]{1,0:T(8,128)(2,1)S(1)} %pad_maximum_fusion.refs_0_), channel_id=1, source_target_pairs={{0,4},{1,5},{2,6},{3,7},{4,0},{5,1},{6,2},{7,3},{8,12},{9,13},{10,... | collective-permute-start | bytes 712712 | tf_op jit(solution)/shard_map/ppermute | solution.py:136
  16.4 10.2 %collective-permute-start.3 = (bf16[32,3712]{1,0:T(8,128)(2,1)S(1)}, bf16[32,3712]{1,0:T(8,128)(2,1)S(1)}, u32[]{:S(2)}, u32[]{:S(2)}) collective-permute-start(bf16[32,3712]{1,0:T(8,128)(2,1)S(1)} %pad_maximum_fusion.refs_0_), channel_id=1, source_target_pairs={{0,2},{1,3},{2,0},{3,1},{4,6},{5,7},{6,4},{7,5},{8,10},{9,11},{10,... | collective-permute-start | bytes 712712 | tf_op jit(solution)/shard_map/ppermute | solution.py:136
  16.8 11.1 %collective-permute-start.6 = (bf16[32,3712]{1,0:T(8,128)(2,1)S(1)}, bf16[32,3712]{1,0:T(8,128)(2,1)S(1)}, u32[]{:S(2)}, u32[]{:S(2)}) collective-permute-start(bf16[32,3712]{1,0:T(8,128)(2,1)S(1)} %pad_maximum_fusion.refs_0_), channel_id=1, source_target_pairs={{0,1},{1,0},{2,3},{3,2},{4,5},{5,4},{6,7},{7,6},{8,9},{9,8},{10,11... | collective-permute-start | bytes 712712 | tf_op jit(solution)/shard_map/ppermute | solution.py:136
  22.9 5.0 %collective-permute-start.9 = (bf16[32,3712]{1,0:T(8,128)(2,1)S(1)}, bf16[32,3712]{1,0:T(8,128)(2,1)S(1)}, u32[]{:S(2)}, u32[]{:S(2)}) collective-permute-start(bf16[32,3712]{1,0:T(8,128)(2,1)S(1)} %collective-permute-done.5.refs_3_), channel_id=1, source_target_pairs={{0,1},{1,0},{2,3},{3,2},{4,5},{5,4},{6,7},{7,6},{8,9},{9,8},{10,11... | collective-permute-start | bytes 712712 | tf_op jit(solution)/shard_map/ppermute | solution.py:136
  26.5 1.5 %collective-permute-start.8 = (bf16[32,3712]{1,0:T(8,128)(2,1)S(1)}, bf16[32,3712]{1,0:T(8,128)(2,1)S(1)}, u32[]{:S(2)}, u32[]{:S(2)}) collective-permute-start(bf16[32,3712]{1,0:T(8,128)(2,1)S(1)} %collective-permute-done.4.refs_2_), channel_id=1, source_target_pairs={{0,1},{1,0},{2,3},{3,2},{4,5},{5,4},{6,7},{7,6},{8,9},{9,8},{10,11... | collective-permute-start | bytes 712712 | tf_op jit(solution)/shard_map/ppermute | solution.py:136
  26.6 1.7 %collective-permute-start.7 = (bf16[32,3712]{1,0:T(8,128)(2,1)S(1)}, bf16[32,3712]{1,0:T(8,128)(2,1)S(1)}, u32[]{:S(2)}, u32[]{:S(2)}) collective-permute-start(bf16[32,3712]{1,0:T(8,128)(2,1)S(1)} %collective-permute-done.3.refs_1_), channel_id=1, source_target_pairs={{0,1},{1,0},{2,3},{3,2},{4,5},{5,4},{6,7},{7,6},{8,9},{9,8},{10,11... | collective-permute-start | bytes 712712 | tf_op jit(solution)/shard_map/ppermute | solution.py:136
  28.4 2.0 %copy-start = (bf16[1,3584,512]{2,1,0:T(8,128)(2,1)S(1)}, bf16[1,3584,512]{2,1,0:T(8,128)(2,1)}, u32[]{:S(2)}) copy-start(bf16[1,3584,512]{2,1,0:T(8,128)(2,1)} %param.15) | copy-start | bytes 11010052
  30.4 2.0 %copy-start.1 = (bf16[1,3584,512]{2,1,0:T(8,128)(2,1)S(1)}, bf16[1,3584,512]{2,1,0:T(8,128)(2,1)}, u32[]{:S(2)}) copy-start(bf16[1,3584,512]{2,1,0:T(8,128)(2,1)} %param.16) | copy-start | bytes 11010052
  32.4 2.0 %copy-start.2 = (bf16[1,512,3584]{2,1,0:T(8,128)(2,1)S(1)}, bf16[1,512,3584]{2,1,0:T(8,128)(2,1)}, u32[]{:S(2)}) copy-start(bf16[1,512,3584]{2,1,0:T(8,128)(2,1)} %param.17) | copy-start | bytes 11010052
  34.5 2.0 %copy-start.3 = (bf16[1,2,3584,256]{3,2,1,0:T(8,128)(2,1)S(1)}, bf16[1,2,3584,256]{3,2,1,0:T(8,128)(2,1)}, u32[]{:S(2)}) copy-start(bf16[1,2,3584,256]{3,2,1,0:T(8,128)(2,1)} %param.18) | copy-start | bytes 11010052
  36.5 2.0 %copy-start.4 = (bf16[1,2,256,3584]{3,2,1,0:T(8,128)(2,1)S(1)}, bf16[1,2,256,3584]{3,2,1,0:T(8,128)(2,1)}, u32[]{:S(2)}) copy-start(bf16[1,2,256,3584]{3,2,1,0:T(8,128)(2,1)} %param.19) | copy-start | bytes 11010052
  47.5 1.6 %collective-permute-start.11 = (bf16[32,3584]{1,0:T(8,128)(2,1)S(1)}, bf16[32,3584]{1,0:T(8,128)(2,1)S(1)}, u32[]{:S(2)}, u32[]{:S(2)}) collective-permute-start(bf16[32,3584]{1,0:T(8,128)(2,1)S(1)} %get-tuple-element.16), channel_id=1, source_target_pairs={{0,1},{1,0},{2,3},{3,2},{4,5},{5,4},{6,7},{7,6},{8,9},{9,8},{10,11... | collective-permute-start | bytes 688136 | tf_op jit(solution)/shard_map/ppermute | solution.py:136
  47.8 5.2 %collective-permute-start.10 = (bf16[32,3584]{1,0:T(8,128)(2,1)S(1)}, bf16[32,3584]{1,0:T(8,128)(2,1)S(1)}, u32[]{:S(2)}, u32[]{:S(2)}) collective-permute-start(bf16[32,3584]{1,0:T(8,128)(2,1)S(1)} %get-tuple-element.14), channel_id=1, source_target_pairs={{0,1},{1,0},{2,3},{3,2},{4,5},{5,4},{6,7},{7,6},{8,9},{9,8},{10,11... | collective-permute-start | bytes 688136 | tf_op jit(solution)/shard_map/ppermute | solution.py:136
  48.1 2.6 %collective-permute-start.13 = (bf16[32,3584]{1,0:T(8,128)(2,1)S(1)}, bf16[32,3584]{1,0:T(8,128)(2,1)S(1)}, u32[]{:S(2)}, u32[]{:S(2)}) collective-permute-start(bf16[32,3584]{1,0:T(8,128)(2,1)S(1)} %get-tuple-element.18), channel_id=1, source_target_pairs={{0,1},{1,0},{2,3},{3,2},{4,5},{5,4},{6,7},{7,6},{8,9},{9,8},{10,11... | collective-permute-start | bytes 688136 | tf_op jit(solution)/shard_map/ppermute | solution.py:136
  48.3 3.4 %collective-permute-start.15 = (bf16[32,3584]{1,0:T(8,128)(2,1)S(1)}, bf16[32,3584]{1,0:T(8,128)(2,1)S(1)}, u32[]{:S(2)}, u32[]{:S(2)}) collective-permute-start(bf16[32,3584]{1,0:T(8,128)(2,1)S(1)} %get-tuple-element.20), channel_id=1, source_target_pairs={{0,1},{1,0},{2,3},{3,2},{4,5},{5,4},{6,7},{7,6},{8,9},{9,8},{10,11... | collective-permute-start | bytes 688136 | tf_op jit(solution)/shard_map/ppermute | solution.py:136
  49.2 8.5 %collective-permute-start.12 = (bf16[32,3584]{1,0:T(8,128)(2,1)S(1)}, bf16[32,3584]{1,0:T(8,128)(2,1)S(1)}, u32[]{:S(2)}, u32[]{:S(2)}) collective-permute-start(bf16[32,3584]{1,0:T(8,128)(2,1)S(1)} %add_convert_fusion.3), channel_id=1, source_target_pairs={{0,2},{1,3},{2,0},{3,1},{4,6},{5,7},{6,4},{7,5},{8,10},{9,11},{10,... | collective-permute-start | bytes 688136 | tf_op jit(solution)/shard_map/ppermute | solution.py:136
  50.8 12.4 %collective-permute-start.14 = (bf16[32,3584]{1,0:T(8,128)(2,1)S(1)}, bf16[32,3584]{1,0:T(8,128)(2,1)S(1)}, u32[]{:S(2)}, u32[]{:S(2)}) collective-permute-start(bf16[32,3584]{1,0:T(8,128)(2,1)S(1)} %add_convert_fusion.2), channel_id=1, source_target_pairs={{0,4},{1,5},{2,6},{3,7},{4,0},{5,1},{6,2},{7,3},{8,12},{9,13},{10,... | collective-permute-start | bytes 688136 | tf_op jit(solution)/shard_map/ppermute | solution.py:136
  51.7 11.4 %collective-permute-start.16 = (bf16[32,3584]{1,0:T(8,128)(2,1)S(1)}, bf16[32,3584]{1,0:T(8,128)(2,1)S(1)}, u32[]{:S(2)}, u32[]{:S(2)}) collective-permute-start(bf16[32,3584]{1,0:T(8,128)(2,1)S(1)} %add_convert_fusion.1), channel_id=1, source_target_pairs={{0,6},{1,7},{2,4},{3,5},{4,2},{5,3},{6,0},{7,1},{8,14},{9,15},{10,... | collective-permute-start | bytes 688136 | tf_op jit(solution)/shard_map/ppermute | solution.py:136
  63.3 5.2 %collective-permute-start.17 = (bf16[8,3584]{1,0:T(8,128)(2,1)S(1)}, bf16[8,3584]{1,0:T(8,128)(2,1)S(1)}, u32[]{:S(2)}, u32[]{:S(2)}) collective-permute-start(bf16[8,3584]{1,0:T(8,128)(2,1)S(1)} %get-tuple-element.21), channel_id=1, source_target_pairs={{0,8},{1,9},{2,10},{3,11},{4,12},{5,13},{6,14},{7,15},{8,0},{9,1},... | collective-permute-start | bytes 172040 | tf_op jit(solution)/shard_map/ppermute | solution.py:136
  63.8 6.0 %collective-permute-start.19 = (bf16[8,3584]{1,0:T(8,128)(2,1)S(1)}, bf16[8,3584]{1,0:T(8,128)(2,1)S(1)}, u32[]{:S(2)}, u32[]{:S(2)}) collective-permute-start(bf16[8,3584]{1,0:T(8,128)(2,1)S(1)} %get-tuple-element.22), channel_id=1, source_target_pairs={{0,24},{1,25},{2,26},{3,27},{4,28},{5,29},{6,30},{7,31},{8,16},{9,... | collective-permute-start | bytes 172040 | tf_op jit(solution)/shard_map/ppermute | solution.py:136
  65.7 5.7 %collective-permute-start.18 = (bf16[8,3584]{1,0:T(8,128)(2,1)S(1)}, bf16[8,3584]{1,0:T(8,128)(2,1)S(1)}, u32[]{:S(2)}, u32[]{:S(2)}) collective-permute-start(bf16[8,3584]{1,0:T(8,128)(2,1)S(1)} %get-tuple-element.23), channel_id=1, source_target_pairs={{0,16},{1,17},{2,18},{3,19},{4,20},{5,21},{6,22},{7,23},{8,24},{9,... | collective-permute-start | bytes 172040 | tf_op jit(solution)/shard_map/ppermute | solution.py:136

commit v2 on v1

--- a/solution.py
+++ b/solution.py
@@ -134,6 +134,102 @@
         for e in range(expert_size)
     ]
     return lax.ppermute(value, AXES, pairs)
+
+
+def message_kernel(live_rows, tokens, routes, gates, message, route_tile, gate_tile, sems):
+    rows, width = tokens.shape
+    top = routes.shape[1]
+    copies = [
+        pltpu.make_async_copy(source, target, sems.at[i])
+        for i, (source, target) in enumerate(
+            [(routes, route_tile), (gates, gate_tile), (tokens, message.at[:, :width])]
+        )
+    ]
+    for copy in copies:
+        copy.start()
+    for copy in copies[:2]:
+        copy.wait()
+    live = lax.broadcasted_iota(jnp.int32, (rows, top), 0) < live_rows[0]
+    message[:, width:] = jnp.concatenate(
+        [
+            route_tile[...].astype(jnp.float32),
+            jnp.where(live, gate_tile[...].astype(jnp.float32), 0.0),
+            jnp.zeros((rows, LANES - 2 * top), jnp.float32),
+        ],
+        axis=1,
+    ).astype(jnp.bfloat16)
+    copies[2].wait()
+
+
+def in_hbm(*arrays):
+    return [pltpu.with_memory_space_constraint(a, pltpu.HBM) for a in arrays]
+
+
+def build_message(tokens, routes, gate_values, row_counts):
+    rows, width = tokens.shape
+    return pl.pallas_call(
+        message_kernel,
+        out_shape=pltpu.VMEM((rows, width + LANES), jnp.bfloat16),
+        in_specs=[pl.BlockSpec(memory_space=pltpu.SMEM)]
+        + [pl.BlockSpec(memory_space=pltpu.HBM)] * 3,
+        out_specs=pl.BlockSpec(memory_space=pltpu.VMEM),
+        scratch_shapes=[
+            pltpu.VMEM(routes.shape, routes.dtype),
+            pltpu.VMEM(gate_values.shape, gate_values.dtype),
+            pltpu.SemaphoreType.DMA((3,)),
+        ],
+        compiler_params=pltpu.CompilerParams(vmem_limit_bytes=2 << 20),
+        name="message",
+    )(row_counts, *in_hbm(tokens, routes, gate_values))
+
+
+def fetch_kernel(count, slots_in, *refs):
+    sources, targets = refs[:count], refs[count : 2 * count]
+    ids, slots, sems = refs[2 * count :]
+    ahead = pltpu.make_async_copy(slots_in, slots, sems.at[count])
+    ahead.start()
+    copies = [
+        pltpu.make_async_copy(sources[i].at[0], targets[i], sems.at[i]) for i in range(count)
+    ]
+    for copy in copies:
+        copy.start()
+    ahead.wait()
+    first = lax.axis_index("expert") * JSLOT
+    shift = lax.axis_index("dp") * (JSLOT // lax.axis_size("dp"))
+
+    @pl.loop(0, slots.shape[0])
+    def _(e):
+        place = slots[e] - first
+
+        @pl.when((place >= 0) & (place < JSLOT))
+        def _():
+            ids[(place - shift + JSLOT) % JSLOT] = e.astype(jnp.float32)
+
+    for copy in copies:
+        copy.wait()
+
+
+def fetch(expert_map, weights):
+    count = len(weights)
+    return pl.pallas_call(
+        functools.partial(fetch_kernel, count),
+        out_shape=[pltpu.VMEM(w.shape[1:], w.dtype) for w in weights]
+        + [pltpu.SMEM((JSLOT,), jnp.float32)],
+        in_specs=[pl.BlockSpec(memory_space=pltpu.HBM)] * (count + 1),
+        out_specs=[pl.BlockSpec(memory_space=pltpu.VMEM)] * count
+        + [pl.BlockSpec(memory_space=pltpu.SMEM)],
+        scratch_shapes=[
+            pltpu.SMEM(expert_map.shape, expert_map.dtype),
+            pltpu.SemaphoreType.DMA((count + 1,)),
+        ],
+        compiler_params=pltpu.CompilerParams(vmem_limit_bytes=1 << 20),
+        cost_estimate=pl.CostEstimate(
+            flops=0,
+            bytes_accessed=sum(w.size * w.dtype.itemsize for w in weights),
+            transcendentals=0,
+        ),
+        name="fetch",
+    )(*in_hbm(expert_map, *weights))
 
 
 def ffn_kernel(pieces, ids, *refs):
@@ -216,6 +312,7 @@
             bytes_accessed=2 * width * (2 * hidden + span * rank + inner + 2 * total),
             transcendentals=total * hidden,
         ),
+        name="ffn",
     )(ids, *rows_in, *weights)
 
 
@@ -236,38 +333,22 @@
     delta_out,
 ):
     row_total = tokens.shape[0]
-    top = routes.shape[1]
     dp_size = lax.axis_size("dp")
     expert_size = lax.axis_size("expert")
     chips = expert_size // CORES
-    slot_span = JSLOT // dp_size
 
     def swap(value, dp_bits=0, chip_bits=0, core_bits=0):
         return exchange(value, dp_size, expert_size, dp_bits, chip_bits * CORES + core_bits)
 
-    live = jnp.arange(row_total, dtype=jnp.int32) < row_counts[0]
-    message = jnp.concatenate(
-        [
-            tokens,
-            routes.astype(jnp.bfloat16),
-            jnp.where(live[:, None], gate_values, jnp.bfloat16(0.0)),
-            jnp.zeros((row_total, LANES - 2 * top), jnp.bfloat16),
-        ],
-        axis=1,
-    )
+    message = build_message(tokens, routes, gate_values, row_counts)
     column = jnp.concatenate(
         [message] + [swap(message, dp_bits=k) for k in range(1, dp_size)], axis=0
     )
-    mine = [column] + [swap(column, chip_bits=k) for k in range(1, chips)]
-    theirs = [swap(piece, core_bits=1) for piece in mine]
-
-    first = lax.axis_index("expert") * JSLOT
-    shift = lax.axis_index("dp") * slot_span
-    slots = first + (shift + jnp.arange(JSLOT, dtype=jnp.int32)) % JSLOT
-    experts = jnp.arange(expert_map.shape[0], dtype=jnp.int32)
-    ids = jnp.sum(jnp.where(expert_map[None, :] == slots[:, None], experts[None, :], 0), axis=1)
-    weights = [gate_weight[0], up_weight[0], down_weight[0], delta_in[0], delta_out[0]]
-    partial = ffn(ids.astype(jnp.float32), mine + theirs, weights)
+    *weights, ids = fetch(expert_map, [gate_weight, up_weight, down_weight, delta_in, delta_out])
+    remote = [swap(column, chip_bits=k) for k in range(1, chips)]
+    remote, column, ids = lax.optimization_barrier((remote, column, ids))
+    theirs = [swap(column, core_bits=1)] + [swap(piece, core_bits=1) for piece in remote]
+    partial = ffn(ids, [column] + remote + theirs, weights)
 
     kept, given = partial[:chips], partial[chips:]
     paired = [

time: 72.5 us -> 60.9 us (0.84)
  local copies, waits for them, and re-layouts: 11.1 us -> 0.01 us
  Pallas kernels: 8.97 us -> 15.6 us
  waiting for transfers between devices: 30 us -> 24.6 us
  other arithmetic: 3.3 us -> 1.02 us
    unnamed x10 -> x0, local copies, waits for them, and re-layouts: 10.2 us -> none
    pallas_call x0 -> x2, Pallas kernels: none -> 7.22 us  [the longest x1 6.34 us: fetch(): pl.pallas_call(functools.partial(fetch_kernel, count), out_shape=[pltpu.V...]
    ppermute x20, waiting for transfers between devices: 30 us -> 24.6 us  [exchange(): return lax.ppermute(value, AXES, pairs)]
    concatenate x1 -> x0, local copies, waits for them, and re-layouts: 0.91 us -> none  [dense_body(): jnp.concatenate([tokens, routes.astype(jnp.bfloat16), jnp.where(live[:, N...]
    reduce_sum x1 -> x0, other arithmetic: 0.84 us -> none  [dense_body(): jnp.sum(jnp.where(expert_map[None, :] == slots[:, None], experts[None, :]...]
    select_n x1 -> x0, other arithmetic: 0.75 us -> none  [dense_body(): jnp.where(live[:, None], gate_values, jnp.bfloat16(0.0))]
  transfers between devices with their start and end apart: 20 -> 20, of which waited for: 13 -> 14; matrix products, arithmetic and copies ran while one was open for 1% -> 0% of each run, Pallas kernels for 0% -> 10%
where the time goes in v2:
time: 60.9 us; the launch traced here: 60.7 us
  waiting for transfers between devices  24.6 us (40%)
  starting transfers between devices  18.7 us (31%)
  Pallas kernels  15.6 us (26%)
  other arithmetic  1.02 us (2%)
  between operations  0.73 us (1%)
    ppermute x20, waiting for transfers between devices, exchange(): return lax.ppermute(value, AXES, pairs)  24.6 us
    ppermute x20, starting transfers between devices, exchange(): return lax.ppermute(value, AXES, pairs)  18.7 us
    pallas_call x1, Pallas kernels, ffn(): pl.pallas_call(functools.partial(ffn_kernel, pieces), out_shape=[jax.Shap...  8.4 us
    pallas_call x1, Pallas kernels, fetch(): pl.pallas_call(functools.partial(fetch_kernel, count), out_shape=[pltpu.V...  6.34 us
  transfers between devices with their start and end apart: 20, of which 14 were waited for; matrix products, arithmetic and copies ran while one was open for 0% of the time, Pallas kernels for 10%

profile of v2, /device:TPU:0, one launch (start us, length us, event | category | flops | bytes accessed | tf_op | source)
XLA Modules:
  0.0 60.7 jit_solution(16343389171231475340)
XLA Ops:
  0.7 0.9 %message.1 = bf16[8,3712]{1,0:T(8,128)(2,1)S(1)} custom-call(s32[1]{0:T(128)S(6)} %copy.11.live_rows, bf16[8,3584]{1,0:T(8,128)(2,1)} %tokens.1, s32[8,8]{1,0:T(8,128)} %routes.1, bf16[8,8]{1,0:T(8,128)(2,1)} %gates.1), custom_call_target="tpu_custom_call" | custom-call | tf_op jit(solution)/shard_map/message/pallas_call | solution.py:170
  1.5 5.1 %collective-permute-start.2 = (bf16[8,3712]{1,0:T(8,128)(2,1)S(1)}, bf16[8,3712]{1,0:T(8,128)(2,1)S(1)}, u32[]{:S(2)}, u32[]{:S(2)}) collective-permute-start(bf16[8,3712]{1,0:T(8,128)(2,1)S(1)} %message.1), channel_id=1, source_target_pairs={{0,24},{1,25},{2,26},{3,27},{4,28},{5,29},{6,30},{7,31},{8,16},{9,... | collective-permute-start | bytes 178184 | tf_op jit(solution)/shard_map/ppermute | solution.py:136
  6.7 0.0 collective-permute-start.1
  6.7 0.6 %collective-permute-start = (bf16[8,3712]{1,0:T(8,128)(2,1)S(1)}, bf16[8,3712]{1,0:T(8,128)(2,1)S(1)}, u32[]{:S(2)}, u32[]{:S(2)}) collective-permute-start(bf16[8,3712]{1,0:T(8,128)(2,1)S(1)} %message.1), channel_id=1, source_target_pairs={{0,8},{1,9},{2,10},{3,11},{4,12},{5,13},{6,14},{7,15},{8,0},{9,1},... | collective-permute-start | bytes 178184 | tf_op jit(solution)/shard_map/ppermute | solution.py:136
  7.3 1.7 %collective-permute-done.2 = bf16[8,3712]{1,0:T(8,128)(2,1)S(1)} collective-permute-done((bf16[8,3712]{1,0:T(8,128)(2,1)S(1)}, bf16[8,3712]{1,0:T(8,128)(2,1)S(1)}, u32[]{:S(2)}, u32[]{:S(2)}) %collective-permute-start.2) | collective-permute-done | bytes 59424 | tf_op jit(solution)/shard_map/ppermute | solution.py:136
  9.0 2.8 %collective-permute-done.1 = bf16[8,3712]{1,0:T(8,128)(2,1)S(1)} collective-permute-done((bf16[8,3712]{1,0:T(8,128)(2,1)S(1)}, bf16[8,3712]{1,0:T(8,128)(2,1)S(1)}, u32[]{:S(2)}, u32[]{:S(2)}) %collective-permute-start.1) | collective-permute-done | bytes 59424 | tf_op jit(solution)/shard_map/ppermute | solution.py:136
  11.8 0.0 collective-permute-done
  11.9 2.6 %collective-permute-start.5 = (bf16[32,3712]{1,0:T(8,128)(2,1)S(1)}, bf16[32,3712]{1,0:T(8,128)(2,1)S(1)}, u32[]{:S(2)}, u32[]{:S(2)}) collective-permute-start(bf16[32,3712]{1,0:T(8,128)(2,1)S(1)} %pad_maximum_fusion.refs_0_), channel_id=1, source_target_pairs={{0,6},{1,7},{2,4},{3,5},{4,2},{5,3},{6,0},{7,1},{8,14},{9,15},{10,... | collective-permute-start | bytes 712712 | tf_op jit(solution)/shard_map/ppermute | solution.py:136
  14.5 0.5 collective-permute-start.4
  15.0 0.4 collective-permute-start.3
  15.4 6.3 %fetch.1 = (bf16[3584,512]{1,0:T(8,128)(2,1)S(1)}, bf16[3584,512]{1,0:T(8,128)(2,1)S(1)}, bf16[512,3584]{1,0:T(8,128)(2,1)S(1)}, bf16[2,3584,256]{2,1,0:T(8,128)...) custom-call(s32[64]{0:T(128)} %slots_in.1, bf16[1,3584,512]{2,1,0:T(8,128)(2,1)} %refs_0_.1, ...), custom_call_target="tpu_custom_call" | custom-call | bytes 18350080 | tf_op jit(solution)/shard_map/fetch/pallas_call | solution.py:214
  21.8 0.0 collective-permute-done.5.refs_3_
  21.8 3.3 %collective-permute-done.4.refs_2_ = bf16[32,3712]{1,0:T(8,128)(2,1)S(1)} collective-permute-done((bf16[32,3712]{1,0:T(8,128)(2,1)S(1)}, bf16[32,3712]{1,0:T(8,128)(2,1)S(1)}, u32[]{:S(2)}, u32[]{:S(2)}) %collective-permute-start.4) | collective-permute-done | bytes 237600 | tf_op jit(solution)/shard_map/ppermute | solution.py:136
  25.1 0.1 collective-permute-done.3.refs_1_
  25.2 0.0 collective-permute-start.6
  25.2 0.5 collective-permute-start.7
  25.7 0.0 collective-permute-start.8
  25.7 0.5 collective-permute-start.9
  26.2 0.5 collective-permute-done.6.refs_4_
  26.7 0.3 collective-permute-done.7.refs_5_
  27.1 0.3 collective-permute-done.8.refs_6_
  27.4 0.3 collective-permute-done.9.refs_7_
  27.7 8.4 %ffn.1 = (bf16[32,3584]{1,0:T(8,128)(2,1)S(1)}, bf16[32,3584]{1,0:T(8,128)(2,1)S(1)}, bf16[32,3584]{1,0:T(8,128)(2,1)S(1)}, bf16[32,3584]{1,0:T(8,128)(2,1)S(1)}...) custom-call(f32[8]{0:T(128)S(4)} %get-tuple-element.25.ids, ...), custom_call_target="tpu_custom_call" | custom-call | flops 4697620480 | bytes 22020096 | tf_op jit(solution)/shard_map/ffn/pallas_call | solution.py:299
  36.1 0.2 collective-permute-start.11
  36.4 0.3 collective-permute-start.10
  36.7 0.2 collective-permute-start.13
  36.9 0.3 collective-permute-start.15
  37.2 0.5 collective-permute-done.11
  37.7 0.1 add_convert_fusion.3
  37.8 1.6 %collective-permute-start.12 = (bf16[32,3584]{1,0:T(8,128)(2,1)S(1)}, bf16[32,3584]{1,0:T(8,128)(2,1)S(1)}, u32[]{:S(2)}, u32[]{:S(2)}) collective-permute-start(bf16[32,3584]{1,0:T(8,128)(2,1)S(1)} %add_convert_fusion.3), channel_id=1, source_target_pairs={{0,2},{1,3},{2,0},{3,1},{4,6},{5,7},{6,4},{7,5},{8,10},{9,11},{10,... | collective-permute-start | bytes 688136 | tf_op jit(solution)/shard_map/ppermute | solution.py:136
  39.3 0.0 collective-permute-done.13
  39.3 0.1 add_convert_fusion.2
  39.4 0.8 %collective-permute-start.14 = (bf16[32,3584]{1,0:T(8,128)(2,1)S(1)}, bf16[32,3584]{1,0:T(8,128)(2,1)S(1)}, u32[]{:S(2)}, u32[]{:S(2)}) collective-permute-start(bf16[32,3584]{1,0:T(8,128)(2,1)S(1)} %add_convert_fusion.2), channel_id=1, source_target_pairs={{0,4},{1,5},{2,6},{3,7},{4,0},{5,1},{6,2},{7,3},{8,12},{9,13},{10,... | collective-permute-start | bytes 688136 | tf_op jit(solution)/shard_map/ppermute | solution.py:136
  40.2 0.0 collective-permute-done.15
  40.2 0.1 add_convert_fusion.1
  40.2 1.3 %collective-permute-start.16 = (bf16[32,3584]{1,0:T(8,128)(2,1)S(1)}, bf16[32,3584]{1,0:T(8,128)(2,1)S(1)}, u32[]{:S(2)}, u32[]{:S(2)}) collective-permute-start(bf16[32,3584]{1,0:T(8,128)(2,1)S(1)} %add_convert_fusion.1), channel_id=1, source_target_pairs={{0,6},{1,7},{2,4},{3,5},{4,2},{5,3},{6,0},{7,1},{8,14},{9,15},{10,... | collective-permute-start | bytes 688136 | tf_op jit(solution)/shard_map/ppermute | solution.py:136
  41.6 0.0 collective-permute-done.10
  41.6 4.7 %collective-permute-done.12 = bf16[32,3584]{1,0:T(8,128)(2,1)S(1)} collective-permute-done((bf16[32,3584]{1,0:T(8,128)(2,1)S(1)}, bf16[32,3584]{1,0:T(8,128)(2,1)S(1)}, u32[]{:S(2)}, u32[]{:S(2)}) %collective-permute-start.12) | collective-permute-done | bytes 229408 | tf_op jit(solution)/shard_map/ppermute | solution.py:136
  46.3 5.5 %collective-permute-done.14 = bf16[32,3584]{1,0:T(8,128)(2,1)S(1)} collective-permute-done((bf16[32,3584]{1,0:T(8,128)(2,1)S(1)}, bf16[32,3584]{1,0:T(8,128)(2,1)S(1)}, u32[]{:S(2)}, u32[]{:S(2)}) %collective-permute-start.14) | collective-permute-done | bytes 229408 | tf_op jit(solution)/shard_map/ppermute | solution.py:136
  51.8 0.0 collective-permute-done.16
  51.8 0.2 add_convert_fusion
  52.0 0.4 collective-permute-start.17
  52.4 2.0 %collective-permute-start.19 = (bf16[8,3584]{1,0:T(8,128)(2,1)S(1)}, bf16[8,3584]{1,0:T(8,128)(2,1)S(1)}, u32[]{:S(2)}, u32[]{:S(2)}) collective-permute-start(bf16[8,3584]{1,0:T(8,128)(2,1)S(1)} %get-tuple-element.44), channel_id=1, source_target_pairs={{0,24},{1,25},{2,26},{3,27},{4,28},{5,29},{6,30},{7,31},{8,16},{9,... | collective-permute-start | bytes 172040 | tf_op jit(solution)/shard_map/ppermute | solution.py:136
  54.4 1.1 %collective-permute-start.18 = (bf16[8,3584]{1,0:T(8,128)(2,1)S(1)}, bf16[8,3584]{1,0:T(8,128)(2,1)S(1)}, u32[]{:S(2)}, u32[]{:S(2)}) collective-permute-start(bf16[8,3584]{1,0:T(8,128)(2,1)S(1)} %get-tuple-element.45), channel_id=1, source_target_pairs={{0,16},{1,17},{2,18},{3,19},{4,20},{5,21},{6,22},{7,23},{8,24},{9,... | collective-permute-start | bytes 172040 | tf_op jit(solution)/shard_map/ppermute | solution.py:136
  55.5 1.6 %collective-permute-done.17 = bf16[8,3584]{1,0:T(8,128)(2,1)S(1)} collective-permute-done((bf16[8,3584]{1,0:T(8,128)(2,1)S(1)}, bf16[8,3584]{1,0:T(8,128)(2,1)S(1)}, u32[]{:S(2)}, u32[]{:S(2)}) %collective-permute-start.17) | collective-permute-done | bytes 57376 | tf_op jit(solution)/shard_map/ppermute | solution.py:136
  57.1 1.2 %collective-permute-done.19 = bf16[8,3584]{1,0:T(8,128)(2,1)S(1)} collective-permute-done((bf16[8,3584]{1,0:T(8,128)(2,1)S(1)}, bf16[8,3584]{1,0:T(8,128)(2,1)S(1)}, u32[]{:S(2)}, u32[]{:S(2)}) %collective-permute-start.19) | collective-permute-done | bytes 57376 | tf_op jit(solution)/shard_map/ppermute | solution.py:136
  58.4 1.7 %collective-permute-done.18 = bf16[8,3584]{1,0:T(8,128)(2,1)S(1)} collective-permute-done((bf16[8,3584]{1,0:T(8,128)(2,1)S(1)}, bf16[8,3584]{1,0:T(8,128)(2,1)S(1)}, u32[]{:S(2)}, u32[]{:S(2)}) %collective-permute-start.18) | collective-permute-done | bytes 57376 | tf_op jit(solution)/shard_map/ppermute | solution.py:136
  60.1 0.7 %add_convert_fusion.5 = bf16[8,3584]{1,0:T(8,128)(2,1)} fusion(bf16[8,3584]{1,0:T(8,128)(2,1)S(1)} %collective-permute-done.19, bf16[8,3584]{1,0:T(8,128)(2,1)S(1)} %collective-permute-done.18, bf16[8,3584]{1,0:T(8,128)(2,1)S(1)} %collective-permute-done.17, bf16[32,3584]{1,0:T(8,128)(2,1)S(1)} %add_convert_fusion), kind=kLoop, calls=%fused_computation.6 | loop fusion | flops 229376 | bytes 286720 | tf_op jit(solution)/shard_map/convert_element_type | solution.py:361
  (2 shorter events, 0.0 us)
Async XLA Ops:
  1.5 7.5 %collective-permute-start.2 = (bf16[8,3712]{1,0:T(8,128)(2,1)S(1)}, bf16[8,3712]{1,0:T(8,128)(2,1)S(1)}, u32[]{:S(2)}, u32[]{:S(2)}) collective-permute-start(bf16[8,3712]{1,0:T(8,128)(2,1)S(1)} %message.1), channel_id=1, source_target_pairs={{0,24},{1,25},{2,26},{3,27},{4,28},{5,29},{6,30},{7,31},{8,16},{9,... | collective-permute-start | bytes 178184 | tf_op jit(solution)/shard_map/ppermute | solution.py:136
  6.7 5.2 %collective-permute-start.1 = (bf16[8,3712]{1,0:T(8,128)(2,1)S(1)}, bf16[8,3712]{1,0:T(8,128)(2,1)S(1)}, u32[]{:S(2)}, u32[]{:S(2)}) collective-permute-start(bf16[8,3712]{1,0:T(8,128)(2,1)S(1)} %message.1), channel_id=1, source_target_pairs={{0,16},{1,17},{2,18},{3,19},{4,20},{5,21},{6,22},{7,23},{8,24},{9,... | collective-permute-start | bytes 178184 | tf_op jit(solution)/shard_map/ppermute | solution.py:136
  6.7 5.2 %collective-permute-start = (bf16[8,3712]{1,0:T(8,128)(2,1)S(1)}, bf16[8,3712]{1,0:T(8,128)(2,1)S(1)}, u32[]{:S(2)}, u32[]{:S(2)}) collective-permute-start(bf16[8,3712]{1,0:T(8,128)(2,1)S(1)} %message.1), channel_id=1, source_target_pairs={{0,8},{1,9},{2,10},{3,11},{4,12},{5,13},{6,14},{7,15},{8,0},{9,1},... | collective-permute-start | bytes 178184 | tf_op jit(solution)/shard_map/ppermute | solution.py:136
  11.9 9.9 %collective-permute-start.5 = (bf16[32,3712]{1,0:T(8,128)(2,1)S(1)}, bf16[32,3712]{1,0:T(8,128)(2,1)S(1)}, u32[]{:S(2)}, u32[]{:S(2)}) collective-permute-start(bf16[32,3712]{1,0:T(8,128)(2,1)S(1)} %pad_maximum_fusion.refs_0_), channel_id=1, source_target_pairs={{0,6},{1,7},{2,4},{3,5},{4,2},{5,3},{6,0},{7,1},{8,14},{9,15},{10,... | collective-permute-start | bytes 712712 | tf_op jit(solution)/shard_map/ppermute | solution.py:136
  14.5 10.6 %collective-permute-start.4 = (bf16[32,3712]{1,0:T(8,128)(2,1)S(1)}, bf16[32,3712]{1,0:T(8,128)(2,1)S(1)}, u32[]{:S(2)}, u32[]{:S(2)}) collective-permute-start(bf16[32,3712]{1,0:T(8,128)(2,1)S(1)} %pad_maximum_fusion.refs_0_), channel_id=1, source_target_pairs={{0,4},{1,5},{2,6},{3,7},{4,0},{5,1},{6,2},{7,3},{8,12},{9,13},{10,... | collective-permute-start | bytes 712712 | tf_op jit(solution)/shard_map/ppermute | solution.py:136
  15.0 10.2 %collective-permute-start.3 = (bf16[32,3712]{1,0:T(8,128)(2,1)S(1)}, bf16[32,3712]{1,0:T(8,128)(2,1)S(1)}, u32[]{:S(2)}, u32[]{:S(2)}) collective-permute-start(bf16[32,3712]{1,0:T(8,128)(2,1)S(1)} %pad_maximum_fusion.refs_0_), channel_id=1, source_target_pairs={{0,2},{1,3},{2,0},{3,1},{4,6},{5,7},{6,4},{7,5},{8,10},{9,11},{10,... | collective-permute-start | bytes 712712 | tf_op jit(solution)/shard_map/ppermute | solution.py:136
  25.2 1.5 %collective-permute-start.6 = (bf16[32,3712]{1,0:T(8,128)(2,1)S(1)}, bf16[32,3712]{1,0:T(8,128)(2,1)S(1)}, u32[]{:S(2)}, u32[]{:S(2)}) collective-permute-start(bf16[32,3712]{1,0:T(8,128)(2,1)S(1)} %pad_maximum_fusion.refs_0_), channel_id=1, source_target_pairs={{0,1},{1,0},{2,3},{3,2},{4,5},{5,4},{6,7},{7,6},{8,9},{9,8},{10,11... | collective-permute-start | bytes 712712 | tf_op jit(solution)/shard_map/ppermute | solution.py:136
  25.2 1.8 %collective-permute-start.7 = (bf16[32,3712]{1,0:T(8,128)(2,1)S(1)}, bf16[32,3712]{1,0:T(8,128)(2,1)S(1)}, u32[]{:S(2)}, u32[]{:S(2)}) collective-permute-start(bf16[32,3712]{1,0:T(8,128)(2,1)S(1)} %collective-permute-done.3.refs_1_), channel_id=1, source_target_pairs={{0,1},{1,0},{2,3},{3,2},{4,5},{5,4},{6,7},{7,6},{8,9},{9,8},{10,11... | collective-permute-start | bytes 712712 | tf_op jit(solution)/shard_map/ppermute | solution.py:136
  25.7 1.7 %collective-permute-start.8 = (bf16[32,3712]{1,0:T(8,128)(2,1)S(1)}, bf16[32,3712]{1,0:T(8,128)(2,1)S(1)}, u32[]{:S(2)}, u32[]{:S(2)}) collective-permute-start(bf16[32,3712]{1,0:T(8,128)(2,1)S(1)} %collective-permute-done.4.refs_2_), channel_id=1, source_target_pairs={{0,1},{1,0},{2,3},{3,2},{4,5},{5,4},{6,7},{7,6},{8,9},{9,8},{10,11... | collective-permute-start | bytes 712712 | tf_op jit(solution)/shard_map/ppermute | solution.py:136
  25.7 2.0 %collective-permute-start.9 = (bf16[32,3712]{1,0:T(8,128)(2,1)S(1)}, bf16[32,3712]{1,0:T(8,128)(2,1)S(1)}, u32[]{:S(2)}, u32[]{:S(2)}) collective-permute-start(bf16[32,3712]{1,0:T(8,128)(2,1)S(1)} %collective-permute-done.5.refs_3_), channel_id=1, source_target_pairs={{0,1},{1,0},{2,3},{3,2},{4,5},{5,4},{6,7},{7,6},{8,9},{9,8},{10,11... | collective-permute-start | bytes 712712 | tf_op jit(solution)/shard_map/ppermute | solution.py:136
  36.1 1.6 %collective-permute-start.11 = (bf16[32,3584]{1,0:T(8,128)(2,1)S(1)}, bf16[32,3584]{1,0:T(8,128)(2,1)S(1)}, u32[]{:S(2)}, u32[]{:S(2)}) collective-permute-start(bf16[32,3584]{1,0:T(8,128)(2,1)S(1)} %get-tuple-element.38), channel_id=1, source_target_pairs={{0,1},{1,0},{2,3},{3,2},{4,5},{5,4},{6,7},{7,6},{8,9},{9,8},{10,11... | collective-permute-start | bytes 688136 | tf_op jit(solution)/shard_map/ppermute | solution.py:136
  36.4 5.2 %collective-permute-start.10 = (bf16[32,3584]{1,0:T(8,128)(2,1)S(1)}, bf16[32,3584]{1,0:T(8,128)(2,1)S(1)}, u32[]{:S(2)}, u32[]{:S(2)}) collective-permute-start(bf16[32,3584]{1,0:T(8,128)(2,1)S(1)} %get-tuple-element.36), channel_id=1, source_target_pairs={{0,1},{1,0},{2,3},{3,2},{4,5},{5,4},{6,7},{7,6},{8,9},{9,8},{10,11... | collective-permute-start | bytes 688136 | tf_op jit(solution)/shard_map/ppermute | solution.py:136
  36.7 2.6 %collective-permute-start.13 = (bf16[32,3584]{1,0:T(8,128)(2,1)S(1)}, bf16[32,3584]{1,0:T(8,128)(2,1)S(1)}, u32[]{:S(2)}, u32[]{:S(2)}) collective-permute-start(bf16[32,3584]{1,0:T(8,128)(2,1)S(1)} %get-tuple-element.40), channel_id=1, source_target_pairs={{0,1},{1,0},{2,3},{3,2},{4,5},{5,4},{6,7},{7,6},{8,9},{9,8},{10,11... | collective-permute-start | bytes 688136 | tf_op jit(solution)/shard_map/ppermute | solution.py:136
  36.9 3.3 %collective-permute-start.15 = (bf16[32,3584]{1,0:T(8,128)(2,1)S(1)}, bf16[32,3584]{1,0:T(8,128)(2,1)S(1)}, u32[]{:S(2)}, u32[]{:S(2)}) collective-permute-start(bf16[32,3584]{1,0:T(8,128)(2,1)S(1)} %get-tuple-element.42), channel_id=1, source_target_pairs={{0,1},{1,0},{2,3},{3,2},{4,5},{5,4},{6,7},{7,6},{8,9},{9,8},{10,11... | collective-permute-start | bytes 688136 | tf_op jit(solution)/shard_map/ppermute | solution.py:136
  37.8 8.5 %collective-permute-start.12 = (bf16[32,3584]{1,0:T(8,128)(2,1)S(1)}, bf16[32,3584]{1,0:T(8,128)(2,1)S(1)}, u32[]{:S(2)}, u32[]{:S(2)}) collective-permute-start(bf16[32,3584]{1,0:T(8,128)(2,1)S(1)} %add_convert_fusion.3), channel_id=1, source_target_pairs={{0,2},{1,3},{2,0},{3,1},{4,6},{5,7},{6,4},{7,5},{8,10},{9,11},{10,... | collective-permute-start | bytes 688136 | tf_op jit(solution)/shard_map/ppermute | solution.py:136
  39.4 12.4 %collective-permute-start.14 = (bf16[32,3584]{1,0:T(8,128)(2,1)S(1)}, bf16[32,3584]{1,0:T(8,128)(2,1)S(1)}, u32[]{:S(2)}, u32[]{:S(2)}) collective-permute-start(bf16[32,3584]{1,0:T(8,128)(2,1)S(1)} %add_convert_fusion.2), channel_id=1, source_target_pairs={{0,4},{1,5},{2,6},{3,7},{4,0},{5,1},{6,2},{7,3},{8,12},{9,13},{10,... | collective-permute-start | bytes 688136 | tf_op jit(solution)/shard_map/ppermute | solution.py:136
  40.2 11.5 %collective-permute-start.16 = (bf16[32,3584]{1,0:T(8,128)(2,1)S(1)}, bf16[32,3584]{1,0:T(8,128)(2,1)S(1)}, u32[]{:S(2)}, u32[]{:S(2)}) collective-permute-start(bf16[32,3584]{1,0:T(8,128)(2,1)S(1)} %add_convert_fusion.1), channel_id=1, source_target_pairs={{0,6},{1,7},{2,4},{3,5},{4,2},{5,3},{6,0},{7,1},{8,14},{9,15},{10,... | collective-permute-start | bytes 688136 | tf_op jit(solution)/shard_map/ppermute | solution.py:136
  52.0 5.2 %collective-permute-start.17 = (bf16[8,3584]{1,0:T(8,128)(2,1)S(1)}, bf16[8,3584]{1,0:T(8,128)(2,1)S(1)}, u32[]{:S(2)}, u32[]{:S(2)}) collective-permute-start(bf16[8,3584]{1,0:T(8,128)(2,1)S(1)} %get-tuple-element.43), channel_id=1, source_target_pairs={{0,8},{1,9},{2,10},{3,11},{4,12},{5,13},{6,14},{7,15},{8,0},{9,1},... | collective-permute-start | bytes 172040 | tf_op jit(solution)/shard_map/ppermute | solution.py:136
  52.4 6.0 %collective-permute-start.19 = (bf16[8,3584]{1,0:T(8,128)(2,1)S(1)}, bf16[8,3584]{1,0:T(8,128)(2,1)S(1)}, u32[]{:S(2)}, u32[]{:S(2)}) collective-permute-start(bf16[8,3584]{1,0:T(8,128)(2,1)S(1)} %get-tuple-element.44), channel_id=1, source_target_pairs={{0,24},{1,25},{2,26},{3,27},{4,28},{5,29},{6,30},{7,31},{8,16},{9,... | collective-permute-start | bytes 172040 | tf_op jit(solution)/shard_map/ppermute | solution.py:136
  54.4 5.7 %collective-permute-start.18 = (bf16[8,3584]{1,0:T(8,128)(2,1)S(1)}, bf16[8,3584]{1,0:T(8,128)(2,1)S(1)}, u32[]{:S(2)}, u32[]{:S(2)}) collective-permute-start(bf16[8,3584]{1,0:T(8,128)(2,1)S(1)} %get-tuple-element.45), channel_id=1, source_target_pairs={{0,16},{1,17},{2,18},{3,19},{4,20},{5,21},{6,22},{7,23},{8,24},{9,... | collective-permute-start | bytes 172040 | tf_op jit(solution)/shard_map/ppermute | solution.py:136
